TPU v7x, 32 devices: a whole 2x2x4 slice. The times are simulated.
32 devices in a mesh: ri: 8 (over z, core), rj: 4 (over y, x).
Axes of the slice: x: 2, y: 2, z: 4, core: 2. Of those that a mesh axis runs over, the one named last changes fastest.
Arguments:
- pair: bfloat16 [320, 320, 128], P('ri', 'rj'), may hold values from -6 to 6
- in_gain: float32 [128], replicated, may hold values from 0.1 to 1.9
- in_bias: float32 [128], replicated, may hold values from -3 to 3
- w_in: bfloat16 [128, 512], replicated, may hold values from -0.5 to 0.5
- w_gate: bfloat16 [128, 128], replicated, may hold values from -0.5 to 0.5
- out_gain: float32 [128], replicated, may hold values from 0.1 to 1.9
- out_bias: float32 [128], replicated, may hold values from -3 to 3
- w_out: bfloat16 [128, 128], replicated, may hold values from -0.5 to 0.5
Outputs:
- update: bfloat16 [320, 320, 128], P('ri', 'rj')
All inputs are finite; a program needn't handle non-finite values.
Results may differ from a plain program's by a relative error of at most 0.015.
Values may be sent and summed in bfloat16 or wider, within the bound.
A program may use at most 128 MiB of HBM per device.

v0:
```python
import jax
import jax.numpy as jnp
from jax import lax
from jax.sharding import PartitionSpec as P


def layer_norm(values, gain, bias):
    mean = jnp.mean(values, axis=-1, keepdims=True)
    centered = values - mean
    var = jnp.mean(centered * centered, axis=-1, keepdims=True)
    return centered * lax.rsqrt(var + 1e-05) * gain + bias


def local(pair, in_gain, in_bias, w_in, w_gate, out_gain, out_bias, w_out):
    rows, cols, chans = pair.shape
    hidden = w_out.shape[0]
    normed = layer_norm(pair.astype(jnp.float32), in_gain, in_bias).astype(jnp.bfloat16)
    flat = normed.reshape(rows * cols, chans)
    proj = jnp.dot(flat, w_in, preferred_element_type=jnp.float32)
    a_tile = (
        (jax.nn.sigmoid(proj[:, hidden : 2 * hidden]) * proj[:, :hidden])
        .astype(jnp.bfloat16)
        .reshape(rows, cols, hidden)
    )
    b_tile = (
        (jax.nn.sigmoid(proj[:, 3 * hidden :]) * proj[:, 2 * hidden : 3 * hidden])
        .astype(jnp.bfloat16)
        .reshape(rows, cols, hidden)
    )
    gate = jax.nn.sigmoid(jnp.dot(flat, w_gate, preferred_element_type=jnp.float32)).astype(
        jnp.bfloat16
    )
    a_rows = lax.all_gather(a_tile, "rj", axis=1, tiled=True)
    product = lax.dot_general(
        a_rows, b_tile, (((0,), (0,)), ((2,), (2,))), preferred_element_type=jnp.float32
    )
    summed = lax.psum_scatter(
        jnp.transpose(product, (1, 2, 0)).astype(jnp.bfloat16),
        "ri",
        scatter_dimension=0,
        tiled=True,
    ).astype(jnp.float32)
    tri = summed.reshape(rows * cols, hidden)
    tri_normed = layer_norm(tri, out_gain, out_bias).astype(jnp.bfloat16)
    mixed = jnp.dot(tri_normed, w_out, preferred_element_type=jnp.float32)
    update = gate.astype(jnp.float32) * mixed
    return update.reshape(rows, cols, chans).astype(jnp.bfloat16)


def solution(mesh):
    return jax.shard_map(
        local,
        mesh=mesh,
        in_specs=(P("ri", "rj", None), P(), P(), P(), P(), P(), P(), P()),
        out_specs=P("ri", "rj", None),
        check_vma=False,
    )
```

profile of v0, /device:TPU:0, one launch (start us, length us, event | category | flops | bytes accessed | tf_op | source)
XLA Modules:
  0.0 174.6 jit_solution(12855295967835624654)
XLA Ops:
  6.5 0.0 copy-start
  6.5 0.0 copy-start.1
  6.5 0.0 copy-start.4
  6.5 0.0 copy-start.5
  6.5 0.0 all-gather.2.cloned.1.call-start
  6.6 1.6 convert_reduce_fusion
  8.2 2.3 %fusion.8 = f32[40,80]{1,0:T(8,128)S(1)} fusion(bf16[40,80,128]{2,1,0:T(8,128)(2,1)} %param.8, f32[40,80]{1,0:T(8,128)S(1)} %broadcast_multiply_fusion.1), kind=kLoop, calls=%fused_computation.13 | loop fusion | flops 1635200 | bytes 844800 | tf_op jit(solution)/shard_map/reduce_sum | solution.py:10
  10.6 0.0 copy-done.1
  10.6 0.0 copy-done.4
  10.6 0.0 copy-done.5
  10.6 1.1 fusion.11
  11.7 0.0 copy-done
  11.7 1.0 fusion.24
  12.7 0.9 fusion.12
  13.6 1.1 copy.28
  14.7 0.0 all-gather.2.cloned.1.call-update
  14.7 0.0 reduce-scatter.2.cloned.1.call-start
  14.8 1.6 copy.30
  16.4 46.1 %all-gather.2.cloned.1.call-done = bf16[40,320,128]{2,0,1:T(8,128)(2,1)} async-done(((bf16[40,80,128]{2,0,1:T(8,128)(2,1)}), bf16[40,320,128]{2,0,1:T(8,128)(2,1)}) %all-gather.2.cloned.1.call-update) | async-done | bytes 3276816 | tf_op jit(solution)/shard_map/all_gather | solution.py:33
  62.5 6.7 %copy.29 = bf16[40,320,128]{1,0,2:T(8,128)(2,1)} copy(bf16[40,320,128]{2,0,1:T(8,128)(2,1)} %all-gather.2.cloned.1.call-done) | data formatting | bytes 6553600 | tf_op jit(solution)/shard_map/all_gather | solution.py:33
  69.3 7.4 %convert_bitcast_fusion = bf16[320,80,128]{0,1,2:T(8,128)(2,1)} fusion(bf16[40,320,128]{1,0,2:T(8,128)(2,1)} %copy.29, bf16[40,80,128]{1,0,2:T(8,128)(2,1)S(1)} %copy.30), kind=kOutput, calls=%fused_computation | convolution fusion | flops 265420800 | bytes 10649600 | tf_op jit(solution)/shard_map/dot_general | solution.py:34
  76.7 11.5 %copy.31 = bf16[320,80,128]{2,1,0:T(8,128)(2,1)} copy(bf16[320,80,128]{0,1,2:T(8,128)(2,1)} %convert_bitcast_fusion) | data formatting | bytes 13107200 | tf_op jit(solution)/shard_map/convert_element_type | solution.py:38
  88.2 0.0 copy-start.8
  88.2 0.0 reduce-scatter.2.cloned.1.call-update
  88.2 0.7 copy-done.8
  89.0 0.6 fusion.4
  89.5 0.0 copy-start.6
  89.6 0.0 copy-start.7
  89.6 0.0 copy-start.3
  89.6 71.0 %reduce-scatter.2.cloned.1.call-done = bf16[40,80,128]{2,1,0:T(8,128)(2,1)} async-done(((bf16[320,80,128]{2,1,0:T(8,128)(2,1)}), bf16[40,80,128]{2,1,0:T(8,128)(2,1)}) %reduce-scatter.2.cloned.1.call-update) | async-done | bytes 819216 | tf_op jit(solution)/shard_map/reduce_scatter | solution.py:37
  160.6 0.0 copy-start.2
  160.6 1.6 convert_reduce_fusion.1
  162.2 0.1 div.29
  162.3 2.3 %multiply_reduce_fusion = f32[40,80]{1,0:T(8,128)S(1)} fusion(f32[40,80]{1,0:T(8,128)S(1)} %broadcast_multiply_fusion, bf16[40,80,128]{2,1,0:T(8,128)(2,1)} %reduce-scatter.2.cloned.1.call-done), kind=kLoop, calls=%fused_computation.34 | loop fusion | flops 1635200 | bytes 844800 | tf_op jit(solution)/shard_map/reduce_sum | solution.py:10
  164.7 0.1 rsqrt.21
  164.8 0.0 copy-done.6
  164.8 0.0 copy-done.7
  164.8 0.0 copy-done.2
  164.8 1.7 %fusion.23 = bf16[3200,128]{1,0:T(8,128)(2,1)S(1)} fusion(f32[128]{0:T(128)S(1)} %copy-done.6, f32[128]{0:T(128)S(1)} %copy-done.7, f32[3200]{0:T(1024)S(1)} %rsqrt.21, f32[3200]{0:T(1024)S(1)} %div.29, bf16[40,80,128]{2,1,0:T(8,128)(2,1)S(1)} %copy-done.2), kind=kLoop, calls=%fused_computation.33 | loop fusion | flops 2457600 | bytes 1665024 | tf_op jit(solution)/shard_map/convert_element_type | solution.py:44
  166.5 0.0 copy-done.3
  166.5 1.2 fusion.5
  (4 shorter events, 0.0 us)
Async XLA Ops:
  6.5 5.2 %copy-start = (bf16[128,512]{1,0:T(8,128)(2,1)S(1)}, bf16[128,512]{1,0:T(8,128)(2,1)}, u32[]{:S(2)}) copy-start(bf16[128,512]{1,0:T(8,128)(2,1)} %param.11) | copy-start | bytes 393220
  6.5 4.1 %copy-start.1 = (bf16[40,80,128]{2,1,0:T(8,128)(2,1)S(1)}, bf16[40,80,128]{2,1,0:T(8,128)(2,1)}, u32[]{:S(2)}) copy-start(bf16[40,80,128]{2,1,0:T(8,128)(2,1)} %param.8) | copy-start | bytes 2457604
  6.5 4.1 %copy-start.4 = (f32[128]{0:T(128)S(1)}, f32[128]{0:T(128)}, u32[]{:S(2)}) copy-start(f32[128]{0:T(128)} %param.10) | copy-start | bytes 1540
  6.5 4.1 %copy-start.5 = (f32[128]{0:T(128)S(1)}, f32[128]{0:T(128)}, u32[]{:S(2)}) copy-start(f32[128]{0:T(128)} %param.9) | copy-start | bytes 1540
  6.5 56.0 %all-gather.2.cloned.1.call-start = ((), (), s32[]{:S(2)}) async-start(), calls=%async_computation.1 | async-start | bytes 4096000 | tf_op jit(solution)/shard_map/all_gather | solution.py:33
  14.7 145.9 %reduce-scatter.2.cloned.1.call-start = ((), (), s32[]{:S(2)}) async-start(), calls=%async_computation.2 | async-start | bytes 7372800 | tf_op jit(solution)/shard_map/reduce_scatter | solution.py:37
  88.2 0.8 copy-start.8
  89.5 75.2 %copy-start.6 = (f32[128]{0:T(128)S(1)}, f32[128]{0:T(128)}, u32[]{:S(2)}) copy-start(f32[128]{0:T(128)} %param.14) | copy-start | bytes 1540
  89.6 75.2 %copy-start.7 = (f32[128]{0:T(128)S(1)}, f32[128]{0:T(128)}, u32[]{:S(2)}) copy-start(f32[128]{0:T(128)} %param.13) | copy-start | bytes 1540
  89.6 77.0 %copy-start.3 = (bf16[128,128]{1,0:T(8,128)(2,1)S(1)}, bf16[128,128]{1,0:T(8,128)(2,1)}, u32[]{:S(2)}) copy-start(bf16[128,128]{1,0:T(8,128)(2,1)} %param.15) | copy-start | bytes 98308
  160.6 4.2 %copy-start.2 = (bf16[40,80,128]{2,1,0:T(8,128)(2,1)S(1)}, bf16[40,80,128]{2,1,0:T(8,128)(2,1)}, u32[]{:S(2)}) copy-start(bf16[40,80,128]{2,1,0:T(8,128)(2,1)} %reduce-scatter.2.cloned.1.call-done) | copy-start | bytes 2457604
Sparse Core Ops, SparseCore 0:
  14.8 47.6 all-gather.1
  88.4 72.1 reduce-scatter.1
where the time goes:
time: 175 us
  waiting for transfers between devices  117 us (67%)
  local copies, waits for them, and re-layouts  21.9 us (13%)
  between operations  13.6 us (8%)
  other arithmetic  11.7 us (7%)
  matrix products  10.2 us (6%)
    reduce_scatter x1, waiting for transfers between devices, local(): lax.psum_scatter(jnp.transpose(product, (1, 2, 0)).astype(jnp.bfloat16),...  71 us
    all_gather x1, waiting for transfers between devices, local(): a_rows = lax.all_gather(a_tile, 'rj', axis=1, tiled=True)  46.1 us
    convert_element_type x1, local copies, waits for them, and re-layouts, local(): jnp.transpose(product, (1, 2, 0)).astype(jnp.bfloat16)  11.5 us
    dot_general x1, matrix products, local(): lax.dot_general(a_rows, b_tile, (((0,), (0,)), ((2,), (2,))), preferred_e...  7.43 us
    all_gather x1, local copies, waits for them, and re-layouts, local(): a_rows = lax.all_gather(a_tile, 'rj', axis=1, tiled=True)  6.75 us
    reduce_sum x2, other arithmetic, layer_norm(): var = jnp.mean(centered * centered, axis=-1, keepdims=True)  4.67 us
  transfers between devices with their start and end apart: 2, of which 2 were waited for; matrix products, arithmetic and copies ran while one was open for 1% of the time, Pallas kernels for 0%

commit v1 on v0

--- a/solution.py
+++ b/solution.py
@@ -2,6 +2,24 @@
 import jax.numpy as jnp
 from jax import lax
 from jax.sharding import PartitionSpec as P
+
+
+def joined_along(blocks, dim):
+    shape = list(blocks.shape[1:])
+    shape[dim] *= blocks.shape[0]
+    return jnp.moveaxis(blocks, 0, dim).reshape(shape)
+
+
+def doubled(x, axis):
+    count = lax.axis_size(axis)
+    tiles = x[None]
+    for level in range(count.bit_length() - 1):
+        bit = 1 << level
+        theirs = lax.ppermute(tiles, axis, [(i, i ^ bit) for i in range(count)])
+        both = jnp.stack([tiles, theirs])
+        upper = lax.axis_index(axis) >> level & 1
+        tiles = jnp.where(upper == 0, both, both[::-1]).reshape(-1, *x.shape)
+    return tiles
 
 
 def layer_norm(values, gain, bias):
@@ -30,7 +48,7 @@
     gate = jax.nn.sigmoid(jnp.dot(flat, w_gate, preferred_element_type=jnp.float32)).astype(
         jnp.bfloat16
     )
-    a_rows = lax.all_gather(a_tile, "rj", axis=1, tiled=True)
+    a_rows = joined_along(doubled(a_tile, "rj"), 1)
     product = lax.dot_general(
         a_rows, b_tile, (((0,), (0,)), ((2,), (2,))), preferred_element_type=jnp.float32
     )

time: 175 us -> 190 us (1.086)
  waiting for transfers between devices: 117 us -> 123 us
  starting transfers between devices: 0.08 us -> 4.83 us
  other arithmetic: 11.7 us -> 15.8 us
    ppermute x0 -> x2, waiting for transfers between devices: none -> 51.6 us  [doubled(): theirs = lax.ppermute(tiles, axis, [(i, i ^ bit) for i in range(count)])]
    all_gather x1 -> x0, waiting for transfers between devices: 46.1 us -> none  [local(): a_rows = lax.all_gather(a_tile, 'rj', axis=1, tiled=True)]
    all_gather x1 -> x0, local copies, waits for them, and re-layouts: 6.75 us -> none  [local(): a_rows = lax.all_gather(a_tile, 'rj', axis=1, tiled=True)]
    ppermute x0 -> x2, starting transfers between devices: none -> 4.8 us  [doubled(): theirs = lax.ppermute(tiles, axis, [(i, i ^ bit) for i in range(count)])]
    another operation x0 -> x3, other arithmetic: none -> 3.48 us  [doubled(): both = jnp.stack([tiles, theirs])]
    reshape x1, local copies, waits for them, and re-layouts: 1.1 us -> 4.28 us  [joined_along(): return jnp.moveaxis(blocks, 0, dim).reshape(shape)]
  transfers between devices with their start and end apart: 2 -> 3, of which waited for: 2 -> 3; matrix products, arithmetic and copies ran while one was open for 1% -> 1% of each run, Pallas kernels for 0% -> 0%
where the time goes in v1:
time: 190 us; the launch traced here: 189 us
  waiting for transfers between devices  123 us (65%)
  local copies, waits for them, and re-layouts  21 us (11%)
  other arithmetic  15.8 us (8%)
  between operations  13.6 us (7%)
  matrix products  10.6 us (6%)
  starting transfers between devices  4.83 us (3%)
    reduce_scatter x1, waiting for transfers between devices, local(): lax.psum_scatter(jnp.transpose(product, (1, 2, 0)).astype(jnp.bfloat16),...  71.8 us
    ppermute x2, waiting for transfers between devices, doubled(): theirs = lax.ppermute(tiles, axis, [(i, i ^ bit) for i in range(count)])  51.6 us
    convert_element_type x1, local copies, waits for them, and re-layouts, local(): jnp.transpose(product, (1, 2, 0)).astype(jnp.bfloat16)  11.4 us
    dot_general x1, matrix products, local(): lax.dot_general(a_rows, b_tile, (((0,), (0,)), ((2,), (2,))), preferred_e...  7.81 us
    ppermute x2, starting transfers between devices, doubled(): theirs = lax.ppermute(tiles, axis, [(i, i ^ bit) for i in range(count)])  4.8 us
    reduce_sum x2, other arithmetic, layer_norm(): var = jnp.mean(centered * centered, axis=-1, keepdims=True)  4.67 us
    reshape x1, local copies, waits for them, and re-layouts, joined_along(): return jnp.moveaxis(blocks, 0, dim).reshape(shape)  4.28 us
  transfers between devices with their start and end apart: 3, of which 3 were waited for; matrix products, arithmetic and copies ran while one was open for 1% of the time, Pallas kernels for 0%

profile of v1, /device:TPU:0, one launch (start us, length us, event | category | flops | bytes accessed | tf_op | source)
XLA Modules:
  0.0 189.3 jit_solution(15484176646308829196)
XLA Ops:
  6.5 0.0 copy-start
  6.5 0.0 copy-start.1
  6.5 0.0 copy-start.6
  6.5 0.0 copy-start.7
  6.5 0.0 reduce-scatter.2.cloned.1.call-start
  6.6 1.6 convert_reduce_fusion
  8.2 2.3 %fusion.8 = f32[40,80]{1,0:T(8,128)S(1)} fusion(bf16[40,80,128]{2,1,0:T(8,128)(2,1)} %param.8, f32[40,80]{1,0:T(8,128)S(1)} %broadcast_multiply_fusion.1), kind=kLoop, calls=%fused_computation.16 | loop fusion | flops 1635200 | bytes 844800 | tf_op jit(solution)/shard_map/reduce_sum | solution.py:28
  10.6 0.0 copy-done.1
  10.6 0.0 copy-done.6
  10.6 0.0 copy-done.7
  10.6 1.1 fusion.11
  11.7 0.0 copy-start.3
  11.7 0.9 copy-done.3
  12.6 0.0 copy-done
  12.6 1.0 fusion.26
  13.6 0.9 fusion.12
  14.5 3.0 %collective-permute-start = (bf16[1,40,80,128]{3,2,1,0:T(8,128)(2,1)S(1)}, bf16[1,40,80,128]{3,2,1,0:T(8,128)(2,1)S(1)}, u32[]{:S(2)}, u32[]{:S(2)}) collective-permute-start(bf16[1,40,80,128]{3,2,1,0:T(8,128)(2,1)S(1)} %bitcast.39), channel_id=1, source_target_pairs={{0,1},{1,0},{2,3},{3,2},{4,5},{5,4},{6,7},{7,6},{8,9},{9,8},{10,11... | collective-permute-start | bytes 2457608 | tf_op jit(solution)/shard_map/ppermute | solution.py:18
  17.5 18.2 %collective-permute-done = bf16[1,40,80,128]{3,2,1,0:T(8,128)(2,1)S(1)} collective-permute-done((bf16[1,40,80,128]{3,2,1,0:T(8,128)(2,1)S(1)}, bf16[1,40,80,128]{3,2,1,0:T(8,128)(2,1)S(1)}, u32[]{:S(2)}, u32[]{:S(2)}) %collective-permute-start) | collective-permute-done | bytes 819232 | tf_op jit(solution)/shard_map/ppermute | solution.py:18
  35.7 0.2 pad_maximum_fusion.1
  35.9 1.6 fusion.25
  37.5 1.8 collective-permute-start.1
  39.3 2.1 %copy.31 = bf16[40,80,128]{1,0,2:T(8,128)(2,1)} copy(bf16[40,80,128]{2,1,0:T(8,128)(2,1)S(1)} %bitcast.41) | data formatting | bytes 1638400 | tf_op jit(solution)/shard_map/reshape | solution.py:46
  41.4 33.4 %collective-permute-done.1 = bf16[2,40,80,128]{3,2,1,0:T(8,128)(2,1)} collective-permute-done((bf16[2,40,80,128]{3,2,1,0:T(8,128)(2,1)}, bf16[2,40,80,128]{3,2,1,0:T(8,128)(2,1)}, u32[]{:S(2)}, u32[]{:S(2)}) %collective-permute-start.1) | collective-permute-done | bytes 1638432 | tf_op jit(solution)/shard_map/ppermute | solution.py:18
  74.8 1.7 pad_maximum_fusion
  76.5 0.6 reverse_select_fusion
  77.2 1.0 copy.29
  78.1 4.3 %copy.30 = bf16[40,320,128]{1,0,2:T(8,128)(2,1)} copy(bf16[40,320,128]{2,1,0:T(8,128)(2,1)S(1)} %bitcast.36) | data formatting | bytes 6553600 | tf_op jit(solution)/shard_map/reshape | solution.py:10
  82.4 7.8 %convert_bitcast_fusion = bf16[320,80,128]{0,1,2:T(8,128)(2,1)} fusion(bf16[40,320,128]{1,0,2:T(8,128)(2,1)} %copy.30, bf16[40,80,128]{1,0,2:T(8,128)(2,1)} %copy.31), kind=kOutput, calls=%fused_computation | convolution fusion | flops 265420800 | bytes 10649600 | tf_op jit(solution)/shard_map/dot_general | solution.py:52
  90.2 11.4 %copy.32 = bf16[320,80,128]{2,1,0:T(8,128)(2,1)} copy(bf16[320,80,128]{0,1,2:T(8,128)(2,1)} %convert_bitcast_fusion) | data formatting | bytes 13107200 | tf_op jit(solution)/shard_map/convert_element_type | solution.py:56
  101.7 0.0 copy-start.4
  101.7 0.0 copy-start.10
  101.7 0.0 reduce-scatter.2.cloned.1.call-update
  101.7 1.1 copy-done.4
  102.8 0.0 copy-done.10
  102.8 0.6 fusion.4
  103.4 0.0 copy-start.8
  103.4 0.0 copy-start.9
  103.4 0.0 copy-start.5
  103.4 71.8 %reduce-scatter.2.cloned.1.call-done = bf16[40,80,128]{2,1,0:T(8,128)(2,1)} async-done(((bf16[320,80,128]{2,1,0:T(8,128)(2,1)}), bf16[40,80,128]{2,1,0:T(8,128)(2,1)}) %reduce-scatter.2.cloned.1.call-update) | async-done | bytes 819216 | tf_op jit(solution)/shard_map/reduce_scatter | solution.py:55
  175.3 0.0 copy-start.2
  175.3 1.6 convert_reduce_fusion.1
  176.9 0.1 div.29
  177.0 2.3 %multiply_reduce_fusion = f32[40,80]{1,0:T(8,128)S(1)} fusion(f32[40,80]{1,0:T(8,128)S(1)} %broadcast_multiply_fusion, bf16[40,80,128]{2,1,0:T(8,128)(2,1)} %reduce-scatter.2.cloned.1.call-done), kind=kLoop, calls=%fused_computation.38 | loop fusion | flops 1635200 | bytes 844800 | tf_op jit(solution)/shard_map/reduce_sum | solution.py:28
  179.4 0.1 rsqrt.21
  179.4 0.0 copy-done.8
  179.4 0.0 copy-done.9
  179.5 0.0 copy-done.2
  179.5 1.7 fusion.23
  181.2 0.0 copy-done.5
  181.2 1.3 fusion.5
  (4 shorter events, 0.0 us)
Async XLA Ops:
  6.5 6.1 %copy-start = (bf16[128,512]{1,0:T(8,128)(2,1)S(1)}, bf16[128,512]{1,0:T(8,128)(2,1)}, u32[]{:S(2)}) copy-start(bf16[128,512]{1,0:T(8,128)(2,1)} %param.11) | copy-start | bytes 393220
  6.5 4.1 %copy-start.1 = (bf16[40,80,128]{2,1,0:T(8,128)(2,1)S(1)}, bf16[40,80,128]{2,1,0:T(8,128)(2,1)}, u32[]{:S(2)}) copy-start(bf16[40,80,128]{2,1,0:T(8,128)(2,1)} %param.8) | copy-start | bytes 2457604
  6.5 4.1 %copy-start.6 = (f32[128]{0:T(128)S(1)}, f32[128]{0:T(128)}, u32[]{:S(2)}) copy-start(f32[128]{0:T(128)} %param.10) | copy-start | bytes 1540
  6.5 4.1 %copy-start.7 = (f32[128]{0:T(128)S(1)}, f32[128]{0:T(128)}, u32[]{:S(2)}) copy-start(f32[128]{0:T(128)} %param.9) | copy-start | bytes 1540
  6.5 168.7 %reduce-scatter.2.cloned.1.call-start = ((), (), s32[]{:S(2)}) async-start(), calls=%async_computation.1 | async-start | bytes 7372800 | tf_op jit(solution)/shard_map/reduce_scatter | solution.py:55
  11.7 0.9 copy-start.3
  14.5 21.3 %collective-permute-start = (bf16[1,40,80,128]{3,2,1,0:T(8,128)(2,1)S(1)}, bf16[1,40,80,128]{3,2,1,0:T(8,128)(2,1)S(1)}, u32[]{:S(2)}, u32[]{:S(2)}) collective-permute-start(bf16[1,40,80,128]{3,2,1,0:T(8,128)(2,1)S(1)} %bitcast.39), channel_id=1, source_target_pairs={{0,1},{1,0},{2,3},{3,2},{4,5},{5,4},{6,7},{7,6},{8,9},{9,8},{10,11... | collective-permute-start | bytes 2457608 | tf_op jit(solution)/shard_map/ppermute | solution.py:18
  37.5 37.3 %collective-permute-start.1 = (bf16[2,40,80,128]{3,2,1,0:T(8,128)(2,1)}, bf16[2,40,80,128]{3,2,1,0:T(8,128)(2,1)}, u32[]{:S(2)}, u32[]{:S(2)}) collective-permute-start(bf16[2,40,80,128]{3,2,1,0:T(8,128)(2,1)} %get-tuple-element.8), channel_id=1, source_target_pairs={{0,2},{1,3},{2,0},{3,1},{4,6},{5,7},{6,4},{7,5},{8,10},{9,11},{10,... | collective-permute-start | bytes 4915208 | tf_op jit(solution)/shard_map/ppermute | solution.py:18
  101.7 1.1 copy-start.4
  101.7 1.1 copy-start.10
  103.4 76.1 %copy-start.8 = (f32[128]{0:T(128)S(1)}, f32[128]{0:T(128)}, u32[]{:S(2)}) copy-start(f32[128]{0:T(128)} %param.14) | copy-start | bytes 1540
  103.4 76.0 %copy-start.9 = (f32[128]{0:T(128)S(1)}, f32[128]{0:T(128)}, u32[]{:S(2)}) copy-start(f32[128]{0:T(128)} %param.13) | copy-start | bytes 1540
  103.4 77.8 %copy-start.5 = (bf16[128,128]{1,0:T(8,128)(2,1)S(1)}, bf16[128,128]{1,0:T(8,128)(2,1)}, u32[]{:S(2)}) copy-start(bf16[128,128]{1,0:T(8,128)(2,1)} %param.15) | copy-start | bytes 98308
  175.3 4.2 %copy-start.2 = (bf16[40,80,128]{2,1,0:T(8,128)(2,1)S(1)}, bf16[40,80,128]{2,1,0:T(8,128)(2,1)}, u32[]{:S(2)}) copy-start(bf16[40,80,128]{2,1,0:T(8,128)(2,1)} %reduce-scatter.2.cloned.1.call-done) | copy-start | bytes 2457604
Sparse Core Ops, SparseCore 0:
  101.8 73.4 reduce-scatter.1
